TPU v7x, 256 devices: a whole 4x4x8 slice. The times are simulated.
256 devices in a mesh: seq: 64 (over z, x, core), tp: 4 (over y).
Axes of the slice: x: 4, y: 4, z: 8, core: 2. Of those that a mesh axis runs over, the one named last changes fastest.
Arguments:
- tokens: bfloat16 [32768, 2048], P('seq', 'tp'), may hold values from -6 to 6
- norm_gain: float32 [2048], replicated, may hold values from 0.1 to 1.9
- w_query: bfloat16 [2048, 2048], P(None, 'tp'), may hold values from -0.125 to 0.125
- w_keyval: bfloat16 [2048, 256], replicated, may hold values from -0.125 to 0.125
- w_out: bfloat16 [2048, 2048], P('tp'), may hold values from -0.5 to 0.5
- span_lens: int32 [64], P('seq'), may hold values from 1 to 512, 24576 in all
- cached_lens: int32 [64], P('seq'), may hold values from 1 to 1536, 49152 in all
- old_table: int32 [64, 64], P('seq'), may hold values from 0 to 63, each once within a row
- new_table: int32 [64, 64], P('seq'), may hold values from 0 to 63, each once within a row
- old_cache: bfloat16 [4096, 32, 256], P('seq', 'tp'), may hold values from -720 to 720
Outputs:
- mixed: bfloat16 [32768, 2048], P('seq', 'tp')
- new_cache: bfloat16 [4096, 32, 256], P('seq', 'tp')
Inputs may be any that keep to these rules, and one draw needn't show every extreme that they name: Request r's new tokens are the first span_lens[r] of its 512 rows. `old_table`: each row names every device once: each device holds exactly one block of every request. `new_table`: each row names every device once: each device receives exactly one block of every request.
All inputs are finite; a program needn't handle non-finite values. No bound on the sum of `span_lens` or of `cached_lens` on one device may be relied on, other than what follows from the above.
Results may differ from a plain program's by a relative error of at most 0.012.
The roundings to bfloat16 on the way count: a program that leaves them out, or rounds other values in their place, can miss the bound.
Values may be sent and summed in bfloat16 or wider, within the bound.
A program may use at most 128 MiB of HBM per device.

v0:
```python
import jax
import jax.numpy as jnp
from jax import lax
from jax.sharding import PartitionSpec as P

EPSILON = 1e-05
MASKED = -1e30


def normalize(rows, norm_gain):
    values = rows.astype(jnp.float32)
    average = jnp.mean(values, axis=1, keepdims=True)
    centred = values - average
    spread = jnp.mean(centred * centred, axis=1, keepdims=True)
    return (centred * lax.rsqrt(spread + EPSILON) * norm_gain).astype(jnp.bfloat16)


def body(
    tokens,
    norm_gain,
    w_query,
    w_keyval,
    w_out,
    span_lens,
    cached_lens,
    old_table,
    new_table,
    old_cache,
):
    groups = lax.axis_size("seq")
    tp_count = lax.axis_size("tp")
    tp_index = lax.axis_index("tp")
    holders = old_table[0]
    held_len = cached_lens[0]
    span_len = span_lens[0]
    tok_rows = tokens.shape[0]
    share = old_cache.shape[1]
    width = old_cache.shape[2]
    block_rows = share * tp_count
    capacity = groups * block_rows
    arrived = lax.all_to_all(old_cache, "seq", split_axis=0, concat_axis=0, tiled=True)
    cache_share = jnp.take(arrived, holders, axis=0)
    full_rows = lax.all_gather(tokens, "tp", axis=1, tiled=True)
    normed = normalize(full_rows, norm_gain)
    query = jnp.dot(normed, w_query, preferred_element_type=jnp.float32).astype(jnp.bfloat16)
    keyval = jnp.dot(normed, w_keyval, preferred_element_type=jnp.float32).astype(jnp.bfloat16)
    shifted = lax.dynamic_update_slice(
        jnp.zeros((capacity, width), jnp.bfloat16), keyval, (held_len, jnp.int32(0))
    )
    shifted_share = lax.dynamic_slice_in_dim(
        shifted.reshape(groups, block_rows, width), tp_index * share, share, 1
    )
    share_pos = (
        lax.broadcasted_iota(jnp.int32, (groups, share, 1), 0) * block_rows
        + tp_index * share
        + lax.broadcasted_iota(jnp.int32, (groups, share, 1), 1)
    )
    fresh_share = jnp.where(
        share_pos < held_len,
        cache_share,
        jnp.where(share_pos < held_len + span_len, shifted_share, jnp.zeros_like(shifted_share)),
    )
    targets = new_table[0]
    device_ids = lax.broadcasted_iota(jnp.int32, (groups, groups), 0)
    block_ids = lax.broadcasted_iota(jnp.int32, (groups, groups), 1)
    matches = targets[None, :] == device_ids
    sources = jnp.sum(jnp.where(matches, block_ids, 0), axis=1)
    new_cache = lax.all_to_all(
        jnp.take(fresh_share, sources, axis=0), "seq", split_axis=0, concat_axis=0, tiled=True
    )
    cached = lax.all_gather(cache_share, "tp", axis=1, tiled=True).reshape(capacity, width)
    positions = lax.broadcasted_iota(jnp.int32, (capacity, 1), 0)
    fresh = jnp.where(
        positions < held_len,
        cached,
        jnp.where(positions < held_len + span_len, shifted, jnp.zeros_like(shifted)),
    )
    head_size = width // 2
    keys = fresh[:, :head_size]
    values = fresh[:, head_size:]
    local_heads = query.shape[1] // head_size
    query3 = query.reshape(tok_rows, local_heads, head_size)
    scores = jnp.einsum(
        "thd,kd->htk", query3, keys, preferred_element_type=jnp.float32
    ) * head_size ** (-0.5)
    row_pos = lax.broadcasted_iota(jnp.int32, (tok_rows, 1), 0)
    key_pos = lax.broadcasted_iota(jnp.int32, (1, capacity), 1)
    allowed = key_pos <= held_len + row_pos
    scores = jnp.where(allowed[None], scores, MASKED)
    top = jnp.max(scores, axis=2, keepdims=True)
    weights = jnp.exp(scores - top)
    probs = (weights / jnp.sum(weights, axis=2, keepdims=True)).astype(jnp.bfloat16)
    context = jnp.einsum("htk,kd->thd", probs, values, preferred_element_type=jnp.float32).astype(
        jnp.bfloat16
    )
    context = context.reshape(tok_rows, local_heads * head_size)
    partial_out = jnp.dot(context, w_out, preferred_element_type=jnp.float32)
    summed = lax.psum_scatter(
        partial_out.astype(jnp.bfloat16), "tp", scatter_dimension=1, tiled=True
    ).astype(jnp.float32)
    total = tokens.astype(jnp.float32) + summed
    mixed = jnp.where(row_pos < span_len, total, jnp.zeros_like(total)).astype(jnp.bfloat16)
    return (mixed, new_cache)


def solution(mesh):
    in_specs = (
        P("seq", "tp"),
        P(),
        P(None, "tp"),
        P(),
        P("tp", None),
        P("seq"),
        P("seq"),
        P("seq", None),
        P("seq", None),
        P("seq", "tp", None),
    )
    out_specs = (P("seq", "tp"), P("seq", "tp", None))
    return jax.shard_map(body, mesh=mesh, in_specs=in_specs, out_specs=out_specs, check_vma=False)
```

profile of v0, /device:TPU:1, one launch (start us, length us, event | category | flops | bytes accessed | tf_op | source)
XLA Modules:
  0.0 153.1 jit_solution(9230389170875504754)
XLA Ops:
  7.2 0.0 copy-start
  7.2 0.0 copy-start.5
  7.2 0.0 all-gather.5.cloned.1.call-start
  7.2 0.7 all-gather.5.cloned.1.call-update
  7.9 13.0 %all-to-all-start = ((bf16[64,8,256]{2,1,0:T(8,128)(2,1)}), bf16[64,8,256]{2,1,0:T(8,128)(2,1)S(1)}, u32[]{:S(2)}, u32[]{:S(2)}) async-start(bf16[64,8,256]{2,1,0:T(8,128)(2,1)} %param.21), calls=%async_computation | async-start | bytes 524288 | tf_op jit(solution)/shard_map/all_to_all | solution.py:41
  20.9 0.0 all-gather.3.cloned.1.call-start
  22.3 0.7 compare_select_fusion.1
  23.0 0.7 compare_and_fusion.1
  23.6 0.1 fusion.16
  23.7 10.4 %all-to-all-done = bf16[64,8,256]{2,1,0:T(8,128)(2,1)S(1)} async-done(((bf16[64,8,256]{2,1,0:T(8,128)(2,1)}), bf16[64,8,256]{2,1,0:T(8,128)(2,1)S(1)}, u32[]{:S(2)}, u32[]{:S(2)}) %all-to-all-start) | async-done | bytes 262176 | tf_op jit(solution)/shard_map/all_to_all | solution.py:41
  34.1 1.3 gather_fusion
  35.4 11.7 %all-gather.5.cloned.1.call-done = bf16[512,2048]{1,0:T(8,128)(2,1)} async-done(((bf16[512,512]{1,0:T(8,128)(2,1)}), bf16[512,2048]{1,0:T(8,128)(2,1)}) %all-gather.5.cloned.1.call-update) | async-done | bytes 2097168 | tf_op jit(solution)/shard_map/all_gather | solution.py:43
  47.1 2.1 %convert_reduce_fusion = f32[512]{0:T(512)S(1)} fusion(bf16[512,2048]{1,0:T(8,128)(2,1)} %all-gather.5.cloned.1.call-done), kind=kLoop, calls=%fused_computation.12 | loop fusion | flops 2096640 | bytes 2099200 | tf_op jit(solution)/shard_map/reduce_sum | solution.py:12
  49.2 2.3 %fusion.8 = f32[512]{0:T(512)S(1)} fusion(bf16[512,2048]{1,0:T(8,128)(2,1)} %all-gather.5.cloned.1.call-done, f32[512]{0:T(512)S(1)} %broadcast_multiply_fusion), kind=kLoop, calls=%fused_computation.15 | loop fusion | flops 4193792 | bytes 2101248 | tf_op jit(solution)/shard_map/reduce_sum | solution.py:14
  51.5 0.0 copy-done.5
  51.5 0.0 copy-done.1
  51.5 0.7 fusion.10
  52.2 0.0 copy-done.6
  52.3 0.0 copy-start.2
  52.3 0.7 convolution_convert_fusion.2
  53.0 0.6 copy-done.2
  53.6 0.1 broadcast.104
  53.7 1.9 %dynamic_update_slice.3 = bf16[2048,256]{1,0:T(8,128)(2,1)S(1)} dynamic-update-slice(bf16[2048,256]{1,0:T(8,128)(2,1)S(1)} %broadcast.104, bf16[512,256]{1,0:T(8,128)(2,1)S(1)} %convolution_convert_fusion.2, s32[]{:T(128)S(6)} %select_n.39, s32[]{:T(128)} %constant.9.clone.1) | dynamic-update-slice | bytes 524292 | tf_op jit(solution)/shard_map/dynamic_update_slice | solution.py:47
  55.6 1.9 %select_select_fusion = (bf16[64,8,256]{2,1,0:T(8,128)(2,1)S(1)}, bf16[64,8,256]{2,1,0:T(8,128)(2,1)}) fusion(bf16[64,32,256]{2,1,0:T(8,128)(2,1)S(1)} %bitcast.57, s32[]{:T(128)S(6)} %select_n.44, pred[64,8]{1,0:T(8,128)(4,1)S(1)} %get-tuple-element.6, pred[64,8]{1,0:T(8,128)(4,1)S(1)} %get-tuple-element.5, bf16[64,8,256]{2,1,0:T(8,128)(2,1)} %gather_fusion, ...), kind=kLoop, calls=%fused_computation.29 | loop fusion | flops 393216 | bytes 1049668 | tf_op jit(solution)/shard_map/jit(_where)/select_n | solution.py:58
  57.5 0.0 all-gather.3.cloned.1.call-update
  57.5 0.2 reduce-scatter.2.cloned.1.call-start
  57.8 1.8 %iota_compare_fusion = pred[512,2048]{0,1:T(8,128)(4,1)} fusion(s32[512]{0:T(512)S(1)} %iota_add_fusion.1), kind=kLoop, calls=%fused_computation.18 | loop fusion | flops 1048576 | bytes 1050624 | tf_op jit(solution)/shard_map/le | solution.py:88
  59.6 4.3 %convolution_convert_fusion.1 = bf16[512,512]{0,1:T(8,128)(2,1)} fusion(bf16[512,2048]{1,0:T(8,128)(2,1)} %copy-done.2, bf16[2048,512]{1,0:T(8,128)(2,1)} %param.14), kind=kOutput, calls=%fused_computation.21 | convolution fusion | flops 1074003968 | bytes 4718592 | tf_op jit(solution)/shard_map/dot_general | solution.py:45
  63.9 21.4 %all-gather.3.cloned.1.call-done = bf16[64,32,256]{2,1,0:T(8,128)(2,1)} async-done(((bf16[64,8,256]{2,1,0:T(8,128)(2,1)}), bf16[64,32,256]{2,1,0:T(8,128)(2,1)}) %all-gather.3.cloned.1.call-update) | async-done | bytes 1048592 | tf_op jit(solution)/shard_map/all_gather | solution.py:71
  85.3 3.8 %bitcast_select_fusion.4 = bf16[2048,256]{1,0:T(8,128)(2,1)} fusion(bf16[64,32,256]{2,1,0:T(8,128)(2,1)} %all-gather.3.cloned.1.call-done, bf16[2048,256]{1,0:T(8,128)(2,1)S(1)} %dynamic_update_slice.3, pred[2048]{0:T(1024)(128)(4,1)S(1)} %get-tuple-element.9, pred[2048]{0:T(1024)(128)(4,1)S(1)} %get-tuple-element.10), kind=kLoop, calls=%fused_computation.24 | loop fusion | flops 1048576 | bytes 3149824 | tf_op jit(solution)/shard_map/jit(_where)/select_n | solution.py:73
  89.1 10.7 %fusion.19 = (f32[4,512]{1,0:T(4,128)S(1)}, f32[4,512,2048]{1,2,0:T(8,128)}) fusion(pred[512,2048]{0,1:T(8,128)(4,1)} %iota_compare_fusion, bf16[512,4,128]{0,2,1:T(8,128)(2,1)} %bitcast.59, bf16[2048,256]{1,0:T(8,128)(2,1)} %bitcast_select_fusion.4), kind=kOutput, calls=%fused_computation.52 | convolution fusion | flops 1090521088 | bytes 18882560 | tf_op jit(solution)/shard_map/sub | solution.py:91
  99.8 0.0 copy-done.4
  99.8 7.0 %fusion.13 = bf16[128,4,512]{2,0,1:T(8,128)(2,1)S(1)} fusion(f32[4,512,2048]{1,2,0:T(8,128)} %get-tuple-element.8, f32[4,512]{1,0:T(4,128)S(1)} %get-tuple-element.7, bf16[2048,256]{1,0:T(8,128)(2,1)S(1)} %copy-done.4), kind=kOutput, calls=%fused_computation.22 | convolution fusion | flops 1082392576 | bytes 17833984 | tf_op jit(solution)/shard_map/htk,kd->thd/dot_general | solution.py:93
  106.8 0.0 copy-start.7
  106.8 0.0 copy-done
  106.9 0.0 copy-start.3
  106.9 2.6 %convolution_convert_fusion = bf16[512,2048]{1,0:T(8,128)(2,1)} fusion(bf16[512,512]{0,1:T(8,128)(2,1)S(1)} %bitcast.60, bf16[512,2048]{1,0:T(8,128)(2,1)S(1)} %copy-done), kind=kOutput, calls=%fused_computation.19 | convolution fusion | flops 1074790400 | bytes 4718592 | tf_op jit(solution)/shard_map/dot_general | solution.py:97
  109.5 0.0 reduce-scatter.2.cloned.1.call-update
  109.5 0.0 copy-done.7
  109.5 0.1 select_reduce_fusion
  109.7 0.6 gather_fusion.1
  110.3 0.8 broadcast_select_fusion
  111.1 11.5 %all-to-all-start.1 = ((bf16[64,8,256]{2,1,0:T(8,128)(2,1)}), bf16[64,8,256]{2,1,0:T(8,128)(2,1)S(1)}, u32[]{:S(2)}, u32[]{:S(2)}) async-start(bf16[64,8,256]{2,1,0:T(8,128)(2,1)} %broadcast_select_fusion), calls=%async_computation.2 | async-start | bytes 524288 | tf_op jit(solution)/shard_map/all_to_all | solution.py:68
  122.7 13.1 %all-to-all-done.1 = bf16[64,8,256]{2,1,0:T(8,128)(2,1)S(1)} async-done(((bf16[64,8,256]{2,1,0:T(8,128)(2,1)}), bf16[64,8,256]{2,1,0:T(8,128)(2,1)S(1)}, u32[]{:S(2)}, u32[]{:S(2)}) %all-to-all-start.1) | async-done | bytes 262176 | tf_op jit(solution)/shard_map/all_to_all | solution.py:68
  135.8 8.0 %reduce-scatter.2.cloned.1.call-done = bf16[512,512]{1,0:T(8,128)(2,1)} async-done(((bf16[512,2048]{1,0:T(8,128)(2,1)}), bf16[512,512]{1,0:T(8,128)(2,1)}) %reduce-scatter.2.cloned.1.call-update) | async-done | bytes 524304 | tf_op jit(solution)/shard_map/reduce_scatter | solution.py:98
  143.8 0.0 copy-done.3
  143.8 2.0 %select_convert_fusion = bf16[512,512]{1,0:T(8,128)(2,1)} fusion(bf16[512,512]{1,0:T(8,128)(2,1)} %reduce-scatter.2.cloned.1.call-done, bf16[512,512]{1,0:T(8,128)(2,1)S(1)} %copy-done.3, pred[512]{0:T(512)(128)(4,1)S(1)} %iota_compare_fusion.4), kind=kLoop, calls=%fused_computation.25 | loop fusion | flops 1310720 | bytes 1573376 | tf_op jit(solution)/shard_map/convert_element_type | solution.py:102
  145.9 0.7 copy.29
  (13 shorter events, 0.1 us)
Async XLA Ops:
  7.2 99.7 %copy-start = (bf16[512,2048]{1,0:T(8,128)(2,1)S(1)}, bf16[512,2048]{1,0:T(8,128)(2,1)}, u32[]{:S(2)}) copy-start(bf16[512,2048]{1,0:T(8,128)(2,1)} %param.16) | copy-start | bytes 6291460
  7.2 44.3 %copy-start.5 = (f32[2048]{0:T(1024)S(1)}, f32[2048]{0:T(1024)}, u32[]{:S(2)}) copy-start(f32[2048]{0:T(1024)} %param.13) | copy-start | bytes 24580
  7.2 39.9 %all-gather.5.cloned.1.call-start = ((), (), s32[]{:S(2)}) async-start(), calls=%async_computation.4 | async-start | bytes 2621440 | tf_op jit(solution)/shard_map/all_gather | solution.py:43
  7.9 26.2 %all-to-all-start = ((bf16[64,8,256]{2,1,0:T(8,128)(2,1)}), bf16[64,8,256]{2,1,0:T(8,128)(2,1)S(1)}, u32[]{:S(2)}, u32[]{:S(2)}) async-start(bf16[64,8,256]{2,1,0:T(8,128)(2,1)} %param.21), calls=%async_computation | async-start | bytes 524288 | tf_op jit(solution)/shard_map/all_to_all | solution.py:41
  20.9 64.3 %all-gather.3.cloned.1.call-start = ((), (), s32[]{:S(2)}) async-start(), calls=%async_computation.3 | async-start | bytes 1310720 | tf_op jit(solution)/shard_map/all_gather | solution.py:71
  47.1 4.4 %copy-start.1 = (bf16[512,2048]{1,0:T(8,128)(2,1)S(1)}, bf16[512,2048]{1,0:T(8,128)(2,1)}, u32[]{:S(2)}) copy-start(bf16[512,2048]{1,0:T(8,128)(2,1)} %all-gather.5.cloned.1.call-done) | copy-start | bytes 6291460
  47.1 5.1 %copy-start.6 = (bf16[2048,256]{1,0:T(8,128)(2,1)S(1)}, bf16[2048,256]{1,0:T(8,128)(2,1)}, u32[]{:S(2)}) copy-start(bf16[2048,256]{1,0:T(8,128)(2,1)} %param.15) | copy-start | bytes 3145732
  52.3 1.3 copy-start.2
  57.5 86.3 %reduce-scatter.2.cloned.1.call-start = ((), (), s32[]{:S(2)}) async-start(), calls=%async_computation.5 | async-start | bytes 2621440 | tf_op jit(solution)/shard_map/reduce_scatter | solution.py:98
  89.1 10.7 %copy-start.4 = (bf16[2048,256]{1,0:T(8,128)(2,1)S(1)}, bf16[2048,256]{1,0:T(8,128)(2,1)}, u32[]{:S(2)}) copy-start(bf16[2048,256]{1,0:T(8,128)(2,1)} %bitcast_select_fusion.4) | copy-start | bytes 3145732
  106.8 2.7 %copy-start.7 = (s32[1,64]{1,0:T(1,128)S(1)}, s32[1,64]{1,0:T(1,128)}, u32[]{:S(2)}) copy-start(s32[1,64]{1,0:T(1,128)} %param.20) | copy-start | bytes 772
  106.9 37.0 %copy-start.3 = (bf16[512,512]{1,0:T(8,128)(2,1)S(1)}, bf16[512,512]{1,0:T(8,128)(2,1)}, u32[]{:S(2)}) copy-start(bf16[512,512]{1,0:T(8,128)(2,1)} %param.12) | copy-start | bytes 1572868
  111.1 24.7 %all-to-all-start.1 = ((bf16[64,8,256]{2,1,0:T(8,128)(2,1)}), bf16[64,8,256]{2,1,0:T(8,128)(2,1)S(1)}, u32[]{:S(2)}, u32[]{:S(2)}) async-start(bf16[64,8,256]{2,1,0:T(8,128)(2,1)} %broadcast_select_fusion), calls=%async_computation.2 | async-start | bytes 524288 | tf_op jit(solution)/shard_map/all_to_all | solution.py:68
Sparse Core Ops, SparseCore 0:
  9.8 37.2 all-gather.4
  57.6 27.5 all-gather.2
  109.6 34.1 reduce-scatter.1
where the time goes:
time: 154 us; the launch traced here: 153 us
  waiting for transfers between devices  65.4 us (42%)
  matrix products  25.4 us (16%)
  starting transfers between devices  24.8 us (16%)
  other arithmetic  17 us (11%)
  between operations  15.3 us (10%)
  local copies, waits for them, and re-layouts  5.21 us (3%)
    all_gather x1, waiting for transfers between devices, body(): lax.all_gather(cache_share, 'tp', axis=1, tiled=True)  21.4 us
    all_to_all x1, waiting for transfers between devices, body(): lax.all_to_all(jnp.take(fresh_share, sources, axis=0), 'seq', split_axis=...  13.1 us
    all_to_all x1, starting transfers between devices, body(): lax.all_to_all(old_cache, 'seq', split_axis=0, concat_axis=0, tiled=True)  13 us
    all_gather x1, waiting for transfers between devices, body(): full_rows = lax.all_gather(tokens, 'tp', axis=1, tiled=True)  11.7 us
    all_to_all x1, starting transfers between devices, body(): lax.all_to_all(jnp.take(fresh_share, sources, axis=0), 'seq', split_axis=...  11.5 us
    sub x1, matrix products, body(): weights = jnp.exp(scores - top)  10.7 us
    all_to_all x1, waiting for transfers between devices, body(): lax.all_to_all(old_cache, 'seq', split_axis=0, concat_axis=0, tiled=True)  10.4 us
    reduce_scatter x1, waiting for transfers between devices, body(): lax.psum_scatter(partial_out.astype(jnp.bfloat16), 'tp', scatter_dimensio...  8.03 us
  transfers between devices with their start and end apart: 5, of which 5 were waited for; matrix products, arithmetic and copies ran while one was open for 7% of the time, Pallas kernels for 0%

commit v1 on v0

--- a/solution.py
+++ b/solution.py
@@ -40,7 +40,12 @@
     capacity = groups * block_rows
     arrived = lax.all_to_all(old_cache, "seq", split_axis=0, concat_axis=0, tiled=True)
     cache_share = jnp.take(arrived, holders, axis=0)
-    full_rows = lax.all_gather(tokens, "tp", axis=1, tiled=True)
+    ring = [tokens]
+    for hop in range(3):
+        ring.append(lax.ppermute(ring[-1], "tp", [(dev, (dev + 1) % 4) for dev in range(4)]))
+    full_rows = jnp.roll(
+        jnp.concatenate(ring[::-1], axis=1), (lax.axis_index("tp") + 1) * ring[0].shape[1], axis=1
+    )
     normed = normalize(full_rows, norm_gain)
     query = jnp.dot(normed, w_query, preferred_element_type=jnp.float32).astype(jnp.bfloat16)
     keyval = jnp.dot(normed, w_keyval, preferred_element_type=jnp.float32).astype(jnp.bfloat16)

time: 154 us -> 161 us (1.045)
  starting transfers between devices: 24.8 us -> 30.4 us
  local copies, waits for them, and re-layouts: 5.21 us -> 9.3 us
  other arithmetic: 17 us -> 13.6 us
    ppermute x0 -> x3, waiting for transfers between devices: none -> 14.3 us  [body(): lax.ppermute(ring[-1], 'tp', [(dev, (dev + 1) % 4) for dev in range(4)])]
    all_gather x1 -> x0, waiting for transfers between devices: 11.7 us -> none  [body(): full_rows = lax.all_gather(tokens, 'tp', axis=1, tiled=True)]
    ppermute x0 -> x3, starting transfers between devices: none -> 5.13 us  [body(): lax.ppermute(ring[-1], 'tp', [(dev, (dev + 1) % 4) for dev in range(4)])]
    unnamed x17 -> x22, local copies, waits for them, and re-layouts: 1.35 us -> 5.39 us
    all_to_all x1, waiting for transfers between devices: 10.4 us -> 8.21 us  [body(): lax.all_to_all(old_cache, 'seq', split_axis=0, concat_axis=0, tiled=True)]
    reduce_sum x1, other arithmetic: 2.09 us -> 0.36 us  [normalize(): average = jnp.mean(values, axis=1, keepdims=True)]
  transfers between devices with their start and end apart: 5 -> 7, of which waited for: 5 -> 6; matrix products, arithmetic and copies ran while one was open for 7% -> 7% of each run, Pallas kernels for 0% -> 0%
where the time goes in v1:
time: 161 us; the launch traced here: 160 us
  waiting for transfers between devices  65.6 us (41%)
  starting transfers between devices  30.4 us (19%)
  matrix products  25.7 us (16%)
  between operations  15.6 us (10%)
  other arithmetic  13.6 us (8%)
  local copies, waits for them, and re-layouts  9.3 us (6%)
    all_gather x1, waiting for transfers between devices, body(): lax.all_gather(cache_share, 'tp', axis=1, tiled=True)  21.8 us
    ppermute x3, waiting for transfers between devices, body(): lax.ppermute(ring[-1], 'tp', [(dev, (dev + 1) % 4) for dev in range(4)])  14.3 us
    all_to_all x1, starting transfers between devices, body(): lax.all_to_all(old_cache, 'seq', split_axis=0, concat_axis=0, tiled=True)  13.5 us
    all_to_all x1, waiting for transfers between devices, body(): lax.all_to_all(jnp.take(fresh_share, sources, axis=0), 'seq', split_axis=...  13.1 us
    all_to_all x1, starting transfers between devices, body(): lax.all_to_all(jnp.take(fresh_share, sources, axis=0), 'seq', split_axis=...  11.5 us
    sub x1, matrix products, body(): weights = jnp.exp(scores - top)  10.7 us
    all_to_all x1, waiting for transfers between devices, body(): lax.all_to_all(old_cache, 'seq', split_axis=0, concat_axis=0, tiled=True)  8.21 us
    reduce_scatter x1, waiting for transfers between devices, body(): lax.psum_scatter(partial_out.astype(jnp.bfloat16), 'tp', scatter_dimensio...  8.16 us
  transfers between devices with their start and end apart: 7, of which 6 were waited for; matrix products, arithmetic and copies ran while one was open for 7% of the time, Pallas kernels for 0%

profile of v1, /device:TPU:1, one launch (start us, length us, event | category | flops | bytes accessed | tf_op | source)
XLA Modules:
  0.0 160.3 jit_solution(1397621302581382263)
XLA Ops:
  7.2 0.0 copy-start
  7.2 0.0 copy-start.2
  7.2 2.2 %collective-permute-start = (bf16[512,512]{1,0:T(8,128)(2,1)}, bf16[512,512]{1,0:T(8,128)(2,1)S(1)}, u32[]{:S(2)}, u32[]{:S(2)}) collective-permute-start(bf16[512,512]{1,0:T(8,128)(2,1)} %param.12), channel_id=1, source_target_pairs={{0,1},{1,2},{2,3},{3,0},{4,5},{5,6},{6,7},{7,4},{8,9},{9,10},{10,1... | collective-permute-start | bytes 1572872 | tf_op jit(solution)/shard_map/ppermute | solution.py:45
  9.4 11.3 %collective-permute-done = bf16[512,512]{1,0:T(8,128)(2,1)S(1)} collective-permute-done((bf16[512,512]{1,0:T(8,128)(2,1)}, bf16[512,512]{1,0:T(8,128)(2,1)S(1)}, u32[]{:S(2)}, u32[]{:S(2)}) %collective-permute-start) | collective-permute-done | bytes 524320 | tf_op jit(solution)/shard_map/ppermute | solution.py:45
  20.7 1.6 collective-permute-start.1
  22.2 13.5 %all-to-all-start = ((bf16[64,8,256]{2,1,0:T(8,128)(2,1)}), bf16[64,8,256]{2,1,0:T(8,128)(2,1)S(1)}, u32[]{:S(2)}, u32[]{:S(2)}) async-start(bf16[64,8,256]{2,1,0:T(8,128)(2,1)} %param.21), calls=%async_computation | async-start | bytes 524288 | tf_op jit(solution)/shard_map/all_to_all | solution.py:41
  35.7 0.0 all-gather.2.cloned.1.call-start
  37.1 0.8 select_reduce_fusion
  37.8 0.7 compare_select_fusion
  38.5 1.4 collective-permute-start.2
  39.9 0.7 compare_and_fusion.1
  40.6 0.1 fusion.16
  40.7 8.2 %all-to-all-done = bf16[64,8,256]{2,1,0:T(8,128)(2,1)S(1)} async-done(((bf16[64,8,256]{2,1,0:T(8,128)(2,1)}), bf16[64,8,256]{2,1,0:T(8,128)(2,1)S(1)}, u32[]{:S(2)}, u32[]{:S(2)}) %all-to-all-start) | async-done | bytes 262176 | tf_op jit(solution)/shard_map/all_to_all | solution.py:41
  48.9 1.3 gather_fusion
  50.2 3.0 %collective-permute-done.2 = bf16[512,512]{1,0:T(8,128)(2,1)} collective-permute-done((bf16[512,512]{1,0:T(8,128)(2,1)}, bf16[512,512]{1,0:T(8,128)(2,1)}, u32[]{:S(2)}, u32[]{:S(2)}) %collective-permute-start.2) | collective-permute-done | bytes 524320 | tf_op jit(solution)/shard_map/ppermute | solution.py:45
  53.2 1.1 constant_dynamic-update-slice_fusion.7
  54.3 1.1 constant_dynamic-update-slice_fusion.6
  55.4 0.1 constant_dynamic-update-slice_fusion.5
  55.5 0.1 constant_dynamic-update-slice_fusion.4
  55.5 0.0 copy-start.5
  55.6 1.2 constant_dynamic-update-slice_fusion.3
  56.7 1.1 constant_dynamic-update-slice_fusion.2
  57.8 0.1 constant_dynamic-update-slice_fusion.1
  57.9 0.1 constant_dynamic-update-slice_fusion
  58.0 0.4 convert_reduce_fusion
  58.4 0.7 fusion.8
  59.1 0.8 convolution_convert_fusion.2
  59.9 0.0 copy-done.1
  59.9 0.1 broadcast.105
  60.0 1.9 %dynamic_update_slice.3 = bf16[2048,256]{1,0:T(8,128)(2,1)S(1)} dynamic-update-slice(bf16[2048,256]{1,0:T(8,128)(2,1)S(1)} %broadcast.105, bf16[512,256]{1,0:T(8,128)(2,1)S(1)} %convolution_convert_fusion.2, s32[]{:T(128)S(6)} %select_n.54, s32[]{:T(128)} %constant.21.clone.1) | dynamic-update-slice | bytes 524292 | tf_op jit(solution)/shard_map/dynamic_update_slice | solution.py:52
  61.9 1.9 %select_select_fusion = (bf16[64,8,256]{2,1,0:T(8,128)(2,1)S(1)}, bf16[64,8,256]{2,1,0:T(8,128)(2,1)}) fusion(bf16[64,32,256]{2,1,0:T(8,128)(2,1)S(1)} %bitcast.55, s32[]{:T(128)S(6)} %select_n.59, pred[64,8]{1,0:T(8,128)(4,1)S(1)} %get-tuple-element.6, pred[64,8]{1,0:T(8,128)(4,1)S(1)} %get-tuple-element.5, bf16[64,8,256]{2,1,0:T(8,128)(2,1)} %gather_fusion, ...), kind=kLoop, calls=%fused_computation.29 | loop fusion | flops 393216 | bytes 1049668 | tf_op jit(solution)/shard_map/jit(_where)/select_n | solution.py:63
  63.8 0.0 all-gather.2.cloned.1.call-update
  63.8 0.2 reduce-scatter.2.cloned.1.call-start
  64.1 1.8 %iota_compare_fusion = pred[512,2048]{0,1:T(8,128)(4,1)} fusion(s32[512]{0:T(512)S(1)} %iota_add_fusion.1), kind=kLoop, calls=%fused_computation.18 | loop fusion | flops 1048576 | bytes 1050624 | tf_op jit(solution)/shard_map/le | solution.py:93
  65.9 4.5 %convolution_convert_fusion.1 = bf16[512,512]{0,1:T(8,128)(2,1)} fusion(bf16[2048,512]{1,0:T(8,128)(2,1)} %param.14, f32[2048]{0:T(1024)S(1)} %copy-done.6, f32[512]{0:T(512)S(1)} %add_rsqrt_fusion, f32[512]{0:T(512)S(1)} %broadcast_multiply_fusion, bf16[512,4096]{1,0:T(8,128)(2,1)} %copy-done.1, s32[]{:T(128)S(6)} %select_n.53), kind=kOutput, calls=%fused_computation.21 | convolution fusion | flops 1079246848 | bytes 4730884 | tf_op jit(solution)/shard_map/dot_general | solution.py:50
  70.4 21.8 %all-gather.2.cloned.1.call-done = bf16[64,32,256]{2,1,0:T(8,128)(2,1)} async-done(((bf16[64,8,256]{2,1,0:T(8,128)(2,1)}), bf16[64,32,256]{2,1,0:T(8,128)(2,1)}) %all-gather.2.cloned.1.call-update) | async-done | bytes 1048592 | tf_op jit(solution)/shard_map/all_gather | solution.py:76
  92.1 3.8 %bitcast_select_fusion.4 = bf16[2048,256]{1,0:T(8,128)(2,1)} fusion(bf16[64,32,256]{2,1,0:T(8,128)(2,1)} %all-gather.2.cloned.1.call-done, bf16[2048,256]{1,0:T(8,128)(2,1)S(1)} %dynamic_update_slice.3, pred[2048]{0:T(1024)(128)(4,1)S(1)} %get-tuple-element.11, pred[2048]{0:T(1024)(128)(4,1)S(1)} %get-tuple-element.12), kind=kLoop, calls=%fused_computation.24 | loop fusion | flops 1048576 | bytes 3149824 | tf_op jit(solution)/shard_map/jit(_where)/select_n | solution.py:78
  95.9 10.7 %fusion.21 = (f32[4,512]{1,0:T(4,128)S(1)}, f32[4,512,2048]{1,2,0:T(8,128)}) fusion(pred[512,2048]{0,1:T(8,128)(4,1)} %iota_compare_fusion, bf16[512,4,128]{0,2,1:T(8,128)(2,1)} %bitcast.57, bf16[2048,256]{1,0:T(8,128)(2,1)} %bitcast_select_fusion.4), kind=kOutput, calls=%fused_computation.60 | convolution fusion | flops 1090521088 | bytes 18882560 | tf_op jit(solution)/shard_map/sub | solution.py:96
  106.7 7.0 %fusion.13 = bf16[128,4,512]{2,0,1:T(8,128)(2,1)S(1)} fusion(f32[4,512,2048]{1,2,0:T(8,128)} %get-tuple-element.8, f32[4,512]{1,0:T(4,128)S(1)} %get-tuple-element.7, bf16[2048,256]{1,0:T(8,128)(2,1)S(1)} %copy-done.4), kind=kOutput, calls=%fused_computation.22 | convolution fusion | flops 1082392576 | bytes 17833984 | tf_op jit(solution)/shard_map/htk,kd->thd/dot_general | solution.py:98
  113.7 2.6 %convolution_convert_fusion = bf16[512,2048]{1,0:T(8,128)(2,1)} fusion(bf16[512,512]{0,1:T(8,128)(2,1)S(1)} %bitcast.58, bf16[512,2048]{1,0:T(8,128)(2,1)S(1)} %copy-done), kind=kOutput, calls=%fused_computation.19 | convolution fusion | flops 1074790400 | bytes 4718592 | tf_op jit(solution)/shard_map/dot_general | solution.py:102
  116.4 0.0 reduce-scatter.2.cloned.1.call-update
  116.4 0.6 gather_fusion.1
  117.0 0.8 broadcast_select_fusion
  117.9 11.5 %all-to-all-start.1 = ((bf16[64,8,256]{2,1,0:T(8,128)(2,1)}), bf16[64,8,256]{2,1,0:T(8,128)(2,1)S(1)}, u32[]{:S(2)}, u32[]{:S(2)}) async-start(bf16[64,8,256]{2,1,0:T(8,128)(2,1)} %broadcast_select_fusion), calls=%async_computation.2 | async-start | bytes 524288 | tf_op jit(solution)/shard_map/all_to_all | solution.py:73
  129.4 13.1 %all-to-all-done.1 = bf16[64,8,256]{2,1,0:T(8,128)(2,1)S(1)} async-done(((bf16[64,8,256]{2,1,0:T(8,128)(2,1)}), bf16[64,8,256]{2,1,0:T(8,128)(2,1)S(1)}, u32[]{:S(2)}, u32[]{:S(2)}) %all-to-all-start.1) | async-done | bytes 262176 | tf_op jit(solution)/shard_map/all_to_all | solution.py:73
  142.6 8.2 %reduce-scatter.2.cloned.1.call-done = bf16[512,512]{1,0:T(8,128)(2,1)} async-done(((bf16[512,2048]{1,0:T(8,128)(2,1)}), bf16[512,512]{1,0:T(8,128)(2,1)}) %reduce-scatter.2.cloned.1.call-update) | async-done | bytes 524304 | tf_op jit(solution)/shard_map/reduce_scatter | solution.py:103
  150.7 2.0 %select_convert_fusion = bf16[512,512]{1,0:T(8,128)(2,1)} fusion(bf16[512,512]{1,0:T(8,128)(2,1)} %reduce-scatter.2.cloned.1.call-done, bf16[512,512]{1,0:T(8,128)(2,1)S(1)} %copy-done.3, pred[512]{0:T(512)(128)(4,1)S(1)} %iota_compare_fusion.4), kind=kLoop, calls=%fused_computation.25 | loop fusion | flops 1310720 | bytes 1573376 | tf_op jit(solution)/shard_map/convert_element_type | solution.py:107
  152.7 0.7 copy.36
  (20 shorter events, 0.1 us)
Async XLA Ops:
  7.2 106.5 %copy-start = (bf16[512,2048]{1,0:T(8,128)(2,1)S(1)}, bf16[512,2048]{1,0:T(8,128)(2,1)}, u32[]{:S(2)}) copy-start(bf16[512,2048]{1,0:T(8,128)(2,1)} %param.16) | copy-start | bytes 6291460
  7.2 48.3 %copy-start.2 = (bf16[512,512]{1,0:T(8,128)(2,1)S(1)}, bf16[512,512]{1,0:T(8,128)(2,1)}, u32[]{:S(2)}) copy-start(bf16[512,512]{1,0:T(8,128)(2,1)} %param.12) | copy-start | bytes 1572868
  7.2 13.5 %collective-permute-start = (bf16[512,512]{1,0:T(8,128)(2,1)}, bf16[512,512]{1,0:T(8,128)(2,1)S(1)}, u32[]{:S(2)}, u32[]{:S(2)}) collective-permute-start(bf16[512,512]{1,0:T(8,128)(2,1)} %param.12), channel_id=1, source_target_pairs={{0,1},{1,2},{2,3},{3,0},{4,5},{5,6},{6,7},{7,4},{8,9},{9,10},{10,1... | collective-permute-start | bytes 1572872 | tf_op jit(solution)/shard_map/ppermute | solution.py:45
  20.7 17.9 %collective-permute-start.1 = (bf16[512,512]{1,0:T(8,128)(2,1)S(1)}, bf16[512,512]{1,0:T(8,128)(2,1)}, u32[]{:S(2)}, u32[]{:S(2)}) collective-permute-start(bf16[512,512]{1,0:T(8,128)(2,1)S(1)} %collective-permute-done), channel_id=1, source_target_pairs={{0,1},{1,2},{2,3},{3,0},{4,5},{5,6},{6,7},{7,4},{8,9},{9,10},{10,1... | collective-permute-start | bytes 1572872 | tf_op jit(solution)/shard_map/ppermute | solution.py:45
  22.2 26.7 %all-to-all-start = ((bf16[64,8,256]{2,1,0:T(8,128)(2,1)}), bf16[64,8,256]{2,1,0:T(8,128)(2,1)S(1)}, u32[]{:S(2)}, u32[]{:S(2)}) async-start(bf16[64,8,256]{2,1,0:T(8,128)(2,1)} %param.21), calls=%async_computation | async-start | bytes 524288 | tf_op jit(solution)/shard_map/all_to_all | solution.py:41
  35.7 56.4 %all-gather.2.cloned.1.call-start = ((), (), s32[]{:S(2)}) async-start(), calls=%async_computation.3 | async-start | bytes 1310720 | tf_op jit(solution)/shard_map/all_gather | solution.py:76
  38.5 14.6 %collective-permute-start.2 = (bf16[512,512]{1,0:T(8,128)(2,1)}, bf16[512,512]{1,0:T(8,128)(2,1)}, u32[]{:S(2)}, u32[]{:S(2)}) collective-permute-start(bf16[512,512]{1,0:T(8,128)(2,1)} %collective-permute-done.1), channel_id=1, source_target_pairs={{0,1},{1,2},{2,3},{3,0},{4,5},{5,6},{6,7},{7,4},{8,9},{9,10},{10,1... | collective-permute-start | bytes 1572872 | tf_op jit(solution)/shard_map/ppermute | solution.py:45
  55.5 3.5 %copy-start.5 = (bf16[2048,256]{1,0:T(8,128)(2,1)S(1)}, bf16[2048,256]{1,0:T(8,128)(2,1)}, u32[]{:S(2)}) copy-start(bf16[2048,256]{1,0:T(8,128)(2,1)} %param.15) | copy-start | bytes 3145732
  55.5 3.5 %copy-start.6 = (f32[2048]{0:T(1024)S(1)}, f32[2048]{0:T(1024)}, u32[]{:S(2)}) copy-start(f32[2048]{0:T(1024)} %param.13) | copy-start | bytes 24580
  58.0 1.9 %copy-start.1 = (bf16[512,4096]{1,0:T(8,128)(2,1)}, bf16[512,4096]{1,0:T(8,128)(2,1)S(1)}, u32[]{:S(2)}) copy-start(bf16[512,4096]{1,0:T(8,128)(2,1)S(1)} %constant_dynamic-update-slice_fusion) | copy-start | bytes 12582916
  63.8 86.9 %reduce-scatter.2.cloned.1.call-start = ((), (), s32[]{:S(2)}) async-start(), calls=%async_computation.4 | async-start | bytes 2621440 | tf_op jit(solution)/shard_map/reduce_scatter | solution.py:103
  95.9 10.7 %copy-start.4 = (bf16[2048,256]{1,0:T(8,128)(2,1)S(1)}, bf16[2048,256]{1,0:T(8,128)(2,1)}, u32[]{:S(2)}) copy-start(bf16[2048,256]{1,0:T(8,128)(2,1)} %bitcast_select_fusion.4) | copy-start | bytes 3145732
  113.7 37.0 %copy-start.3 = (bf16[512,512]{1,0:T(8,128)(2,1)S(1)}, bf16[512,512]{1,0:T(8,128)(2,1)}, u32[]{:S(2)}) copy-start(bf16[512,512]{1,0:T(8,128)(2,1)} %param.12) | copy-start | bytes 1572868
  117.9 24.7 %all-to-all-start.1 = ((bf16[64,8,256]{2,1,0:T(8,128)(2,1)}), bf16[64,8,256]{2,1,0:T(8,128)(2,1)S(1)}, u32[]{:S(2)}, u32[]{:S(2)}) async-start(bf16[64,8,256]{2,1,0:T(8,128)(2,1)} %broadcast_select_fusion), calls=%async_computation.2 | async-start | bytes 524288 | tf_op jit(solution)/shard_map/all_to_all | solution.py:73
Sparse Core Ops, SparseCore 0:
  64.0 28.1 all-gather.1
  116.5 34.1 reduce-scatter.1
